TPU v7x, 32 devices: a whole 2x2x4 slice. The times are simulated.
32 devices in a mesh: groups: 2 (over y), expert: 8 (over z, x), dp: 2 (over core).
Axes of the slice: x: 2, y: 2, z: 4, core: 2. Of those that a mesh axis runs over, the one named last changes fastest.
Arguments:
- tokens: bfloat16 [4096, 3584], P(('groups', 'expert', 'dp')), parts along dimension 0, may hold values from -6 to 6
- grad_out: bfloat16 [4096, 3584], P(('groups', 'expert', 'dp')), parts along dimension 0, may hold values from -6 to 6
- routing: int32 [4096, 8], P(('groups', 'expert', 'dp')), parts along dimension 0, may hold values from 0 to 63, as said below
- gates: float32 [4096, 8], P(('groups', 'expert', 'dp')), parts along dimension 0, may hold values from 0.05 to 0.5
- modality: int32 [4096], P(('groups', 'expert', 'dp')), parts along dimension 0, may hold values from 0 to 1, as said below
- hot_experts: int32 [4], P('groups'), parts along dimension 0, may hold values from 0 to 7, as said below
- gate_weight: bfloat16 [16384, 3584], P('expert'), may hold values from -0.09375 to 0.09375
- up_weight: bfloat16 [16384, 3584], P('expert'), may hold values from -0.09375 to 0.09375
- down_weight: bfloat16 [16384, 3584], P('expert'), may hold values from -0.125 to 0.125
Outputs:
- grad_tokens: bfloat16 [4096, 3584], P(('groups', 'expert', 'dp')), parts along dimension 0
- grad_gate: bfloat16 [32768, 3584], P(('groups', 'expert', 'dp')), parts along dimension 0
- grad_up: bfloat16 [32768, 3584], P(('groups', 'expert', 'dp')), parts along dimension 0
- grad_down: bfloat16 [32768, 3584], P(('groups', 'expert', 'dp')), parts along dimension 0
There are 2 independent parts, one for each index of `groups`. A program takes and returns all parts, laid end to end along the dimension named above; an argument that names none is the same for every part. Nothing has to cross between parts.
Inputs may be any that keep to these rules, and one draw needn't show every extreme that they name: `routing`: each token names 8 different experts. Among the 128 tokens of each device, every expert in flight that is not hot is named by exactly 2 text tokens, a text token names at most one expert in flight, an image token names none in flight outside its last 2 entries, and no text token names a hot expert. `modality`: exactly 8 image tokens among the 128 tokens of each device. `hot_experts`: 2 different experts in flight.
All inputs are finite; a program needn't handle non-finite values.
Results may differ from a plain program's by a relative error of at most 0.0061.
Values may be sent and summed in bfloat16 or wider, within the bound.
No kernel may reach another device: no remote copies, remote signals or barrier semaphores. Data moves between devices by JAX's collectives and lax.ppermute only.
A program may use at most 384 MiB of HBM per device.

v0:
```python
import jax
import jax.numpy as jnp
from jax import lax
from jax.sharding import PartitionSpec as P

FLIGHT = 8
HOTCAP = 8


def expert_pass(in_tokens, in_scaled, gate_rows, up_rows, down_rows):
    pre_gate = jnp.einsum("nd,hd->nh", in_tokens, gate_rows, preferred_element_type=jnp.float32)
    pre_up = jnp.einsum("nd,hd->nh", in_tokens, up_rows, preferred_element_type=jnp.float32)
    sigmoid_gate = jax.nn.sigmoid(pre_gate)
    swish_gate = pre_gate * sigmoid_gate
    activated = (swish_gate * pre_up).astype(jnp.bfloat16)
    grad_act = jnp.einsum("nd,hd->nh", in_scaled, down_rows, preferred_element_type=jnp.float32)
    grad_pre_gate = (
        grad_act * pre_up * sigmoid_gate * (1.0 + pre_gate * (1.0 - sigmoid_gate))
    ).astype(jnp.bfloat16)
    grad_pre_up = (grad_act * swish_gate).astype(jnp.bfloat16)
    gate_term = jnp.einsum(
        "nh,nd->hd", grad_pre_gate, in_tokens, preferred_element_type=jnp.float32
    )
    up_term = jnp.einsum("nh,nd->hd", grad_pre_up, in_tokens, preferred_element_type=jnp.float32)
    down_term = jnp.einsum("nh,nd->hd", activated, in_scaled, preferred_element_type=jnp.float32)
    partials = jnp.dot(grad_pre_gate, gate_rows, preferred_element_type=jnp.float32)
    partials = (
        partials + jnp.dot(grad_pre_up, up_rows, preferred_element_type=jnp.float32)
    ).astype(jnp.bfloat16)
    return (partials, (gate_term, up_term, down_term))


def per_device(
    tokens, grad_out, routing, gates, modality, hot_experts, gate_weight, up_weight, down_weight
):
    tok_count, model_width = tokens.shape
    top_count = routing.shape[1]
    hot_count = hot_experts.shape[0]
    devices = lax.axis_size("expert")
    split_count = devices // FLIGHT
    position = lax.broadcasted_iota(jnp.int32, (tok_count, top_count), 1)
    pinned_slot = position - (top_count - hot_count)
    pick_table = pinned_slot[:, :, None] == jnp.arange(hot_count, dtype=jnp.int32)[None, None, :]
    hot_pick = jnp.sum(jnp.where(pick_table, hot_experts[None, None, :], 0), axis=2)
    pinned = (modality[:, None] == 1) & (pinned_slot >= 0)
    chosen = jnp.where(pinned, hot_pick, routing)
    matches = chosen[:, :, None] == jnp.arange(FLIGHT, dtype=jnp.int32)[None, None, :]
    expert_gate = jnp.sum(jnp.where(matches, gates[:, :, None], 0.0), axis=1)
    present = jnp.any(matches, axis=1)
    placed = jnp.cumsum(present.astype(jnp.int32), axis=0) - 1
    slot_ids = jnp.arange(HOTCAP, dtype=jnp.int32)
    chooser = (placed.T[:, None, :] == slot_ids[None, :, None]) & present.T[:, None, :]
    picker = chooser.astype(jnp.bfloat16)
    picked = jnp.einsum("scr,rd->scd", picker, tokens, preferred_element_type=jnp.float32).astype(
        jnp.bfloat16
    )
    picked_grad = jnp.einsum("scr,rd->scd", picker, grad_out, preferred_element_type=jnp.float32)
    slot_gate = jnp.sum(jnp.where(chooser, expert_gate.T[:, None, :], 0.0), axis=2)
    scaled = (picked_grad * slot_gate[:, :, None]).astype(jnp.bfloat16)
    picked, scaled = (picked, scaled)
    send_shape = (devices, HOTCAP, model_width)

    def replicate_rows(block_data):
        widened = jnp.broadcast_to(block_data[:, None], (FLIGHT, split_count, HOTCAP, model_width))
        return widened.reshape(send_shape)

    got_tokens, got_scaled = (
        lax.all_to_all(replicate_rows(picked), "expert", split_axis=0, concat_axis=0, tiled=True),
        lax.all_to_all(replicate_rows(scaled), "expert", split_axis=0, concat_axis=0, tiled=True),
    )
    partials, grad_terms = expert_pass(
        got_tokens.reshape(-1, model_width),
        got_scaled.reshape(-1, model_width),
        gate_weight,
        up_weight,
        down_weight,
    )
    returned = lax.all_to_all(
        partials.reshape(send_shape), "expert", split_axis=0, concat_axis=0, tiled=True
    )
    returned = returned.reshape(FLIGHT, split_count, HOTCAP, model_width)
    grad_tokens = jnp.einsum(
        "fcr,fpcd->rd", chooser.astype(jnp.bfloat16), returned, preferred_element_type=jnp.float32
    )
    summed = (
        lax.psum_scatter(grad_terms[0], "dp", scatter_dimension=0, tiled=True),
        lax.psum_scatter(grad_terms[1], "dp", scatter_dimension=0, tiled=True),
        lax.psum_scatter(grad_terms[2], "dp", scatter_dimension=0, tiled=True),
    )
    return (
        grad_tokens.astype(jnp.bfloat16),
        summed[0].astype(jnp.bfloat16),
        summed[1].astype(jnp.bfloat16),
        summed[2].astype(jnp.bfloat16),
    )


def solution(mesh):
    in_specs = (
        P(("groups", "expert", "dp"), None),
        P(("groups", "expert", "dp"), None),
        P(("groups", "expert", "dp"), None),
        P(("groups", "expert", "dp"), None),
        P(("groups", "expert", "dp")),
        P("groups"),
        P("expert", None),
        P("expert", None),
        P("expert", None),
    )
    out_specs = (
        P(("groups", "expert", "dp"), None),
        P(("groups", "expert", "dp"), None),
        P(("groups", "expert", "dp"), None),
        P(("groups", "expert", "dp"), None),
    )
    return jax.shard_map(
        per_device, mesh=mesh, in_specs=in_specs, out_specs=out_specs, check_vma=False
    )
```

profile of v0, /device:TPU:0, one launch (start us, length us, event | category | flops | bytes accessed | tf_op | source)
XLA Modules:
  0.0 211.0 jit_solution(14166473032863376491)
XLA Ops:
  7.2 0.0 copy-start
  7.2 0.7 broadcast_compare_fusion.1
  7.9 0.7 select_reduce_fusion.2
  8.7 0.8 and_select_fusion
  9.5 0.1 copy.28
  9.6 0.2 reduce_window_sum.11
  9.8 0.0 copy-done
  9.8 1.0 convolution_convert_fusion
  10.9 7.3 %all-to-all-start.1 = ((bf16[8,8,3584]{2,1,0:T(8,128)(2,1)}), bf16[8,8,3584]{2,1,0:T(8,128)(2,1)S(1)}, u32[]{:S(2)}, u32[]{:S(2)}) async-start(bf16[8,8,3584]{2,1,0:T(8,128)(2,1)} %convolution_convert_fusion), calls=%async_computation.1 | async-start | bytes 917504 | tf_op jit(solution)/shard_map/all_to_all | solution.py:68
  18.1 0.7 select_reduce_fusion.1
  18.8 0.1 select_reduce_fusion
  18.9 0.1 copy.31
  19.0 2.2 %fusion.1 = bf16[8,8,3584]{2,1,0:T(8,128)(2,1)} fusion(bf16[128,3584]{1,0:T(8,128)(2,1)} %param.10, f32[8,8]{1,0:T(8,128)S(1)} %copy.31, pred[8,8,128]{2,0,1:T(8,128)(4,1)S(1)} %fusion.22), kind=kOutput, calls=%fused_computation.5 | convolution fusion | flops 59179008 | bytes 1384704 | tf_op jit(solution)/shard_map/scr,rd->scd/dot_general | solution.py:57
  21.2 10.0 %all-to-all-done.1 = bf16[8,8,3584]{2,1,0:T(8,128)(2,1)S(1)} async-done(((bf16[8,8,3584]{2,1,0:T(8,128)(2,1)}), bf16[8,8,3584]{2,1,0:T(8,128)(2,1)S(1)}, u32[]{:S(2)}, u32[]{:S(2)}) %all-to-all-start.1) | async-done | bytes 458784 | tf_op jit(solution)/shard_map/all_to_all | solution.py:68
  31.2 3.6 %all-to-all-start = ((bf16[8,8,3584]{2,1,0:T(8,128)(2,1)}), bf16[8,8,3584]{2,1,0:T(8,128)(2,1)S(1)}, u32[]{:S(2)}, u32[]{:S(2)}) async-start(bf16[8,8,3584]{2,1,0:T(8,128)(2,1)} %fusion.1), calls=%async_computation | async-start | bytes 917504 | tf_op jit(solution)/shard_map/all_to_all | solution.py:69
  34.9 0.0 reduce-scatter.8.cloned.1.call-start
  34.9 9.7 %fusion.11 = f32[64,2048]{1,0:T(8,128)S(1)} fusion(bf16[2048,3584]{1,0:T(8,128)(2,1)} %param.15, bf16[8,8,3584]{2,1,0:T(8,128)(2,1)S(1)} %all-to-all-done.1), kind=kOutput, calls=%fused_computation.19 | convolution fusion | flops 939524096 | bytes 15663104 | tf_op jit(solution)/shard_map/nd,hd->nh/dot_general | solution.py:11
  44.6 9.7 %fusion.13 = f32[64,2048]{1,0:T(8,128)S(1)} fusion(bf16[2048,3584]{1,0:T(8,128)(2,1)} %param.16, bf16[8,8,3584]{2,1,0:T(8,128)(2,1)S(1)} %all-to-all-done.1), kind=kOutput, calls=%fused_computation.21 | convolution fusion | flops 939524096 | bytes 15663104 | tf_op jit(solution)/shard_map/nd,hd->nh/dot_general | solution.py:12
  54.2 0.0 all-to-all-done
  54.2 11.7 %fusion.15 = f32[2048,3584]{1,0:T(8,128)} fusion(bf16[8,8,3584]{2,1,0:T(8,128)(2,1)S(1)} %all-to-all-done, f32[64,2048]{1,0:T(8,128)S(1)} %fusion.13, f32[64,2048]{1,0:T(8,128)S(1)} %fusion.11), kind=kOutput, calls=%fused_computation.23 | convolution fusion | flops 940310528 | bytes 30867456 | tf_op jit(solution)/shard_map/nh,nd->hd/dot_general | solution.py:25
  65.9 0.0 reduce-scatter.8.cloned.1.call-update
  66.0 0.0 reduce-scatter.6.cloned.1.call-start
  66.0 9.7 %multiply_convert_fusion.1 = (bf16[64,2048]{1,0:T(8,128)(2,1)S(1)}, bf16[64,2048]{1,0:T(8,128)(2,1)S(1)}) fusion(f32[64,2048]{1,0:T(8,128)S(1)} %fusion.11, f32[64,2048]{1,0:T(8,128)S(1)} %fusion.13, bf16[2048,3584]{1,0:T(8,128)(2,1)} %param.17, bf16[8,8,3584]{2,1,0:T(8,128)(2,1)S(1)} %all-to-all-done), kind=kOutput, calls=%fused_computation.11 | convolution fusion | flops 941228032 | bytes 16711680 | tf_op jit(solution)/shard_map/nd,hd->nh/dot_general | solution.py:16
  75.7 19.1 %fusion.7 = f32[2048,3584]{1,0:T(8,128)} fusion(bf16[64,2048]{1,0:T(8,128)(2,1)S(1)} %get-tuple-element.4, bf16[8,8,3584]{2,1,0:T(8,128)(2,1)S(1)} %all-to-all-done.1), kind=kOutput, calls=%fused_computation.15 | convolution fusion | flops 939524096 | bytes 30081024 | tf_op jit(solution)/shard_map/nh,nd->hd/dot_general | solution.py:24
  94.8 0.0 reduce-scatter.6.cloned.1.call-update
  94.9 0.2 reduce-scatter.4.cloned.1.call-start
  95.1 15.1 %fusion.9 = f32[2048,3584]{1,0:T(8,128)} fusion(bf16[64,2048]{1,0:T(8,128)(2,1)S(1)} %get-tuple-element.5, bf16[8,8,3584]{2,1,0:T(8,128)(2,1)S(1)} %all-to-all-done.1), kind=kOutput, calls=%fused_computation.17 | convolution fusion | flops 939524096 | bytes 30081024 | tf_op jit(solution)/shard_map/nh,nd->hd/dot_general | solution.py:21
  110.2 0.0 reduce-scatter.4.cloned.1.call-update
  110.2 7.8 %fusion.27 = f32[64,3584]{1,0:T(8,128)S(1)} fusion(bf16[64,2048]{1,0:T(8,128)(2,1)S(1)} %get-tuple-element.5, bf16[2048,3584]{1,0:T(8,128)(2,1)} %param.15), kind=kOutput, calls=%fused_computation.44 | convolution fusion | flops 939524096 | bytes 15859712 | tf_op jit(solution)/shard_map/dot_general | solution.py:26
  118.0 10.4 %fusion.3 = bf16[8,8,3584]{2,1,0:T(8,128)(2,1)S(1)} fusion(f32[64,3584]{1,0:T(8,128)S(1)} %fusion.27, bf16[64,2048]{1,0:T(8,128)(2,1)S(1)} %get-tuple-element.4, bf16[2048,3584]{1,0:T(8,128)(2,1)} %param.16), kind=kOutput, calls=%fused_computation.7 | convolution fusion | flops 939982848 | bytes 16318464 | tf_op jit(solution)/shard_map/dot_general | solution.py:28
  128.4 18.5 %all_to_all.15 = bf16[8,8,3584]{2,1,0:T(8,128)(2,1)S(1)} all-to-all(bf16[8,8,3584]{2,1,0:T(8,128)(2,1)S(1)} %fusion.3), channel_id=1, replica_groups=mesh['groups'=2,'expert'=8,'dp'=2] {'expert'}, dimensions={0} | all-to-all | bytes 917504 | tf_op jit(solution)/shard_map/all_to_all | solution.py:78
  146.9 1.4 fusion
  148.3 0.0 reduce-scatter.8.cloned.1.call-done
  148.3 9.6 %convert_element_type.46 = bf16[1024,3584]{1,0:T(8,128)(2,1)} convert(f32[1024,3584]{1,0:T(8,128)} %reduce-scatter.8.cloned.1.call-done) | non-fusion elementwise | flops 3670016 | bytes 22020096 | tf_op jit(solution)/shard_map/convert_element_type | solution.py:94
  157.9 0.0 reduce-scatter.6.cloned.1.call-done
  157.9 0.0 copy-start.1
  157.9 12.1 %convert_element_type.44 = bf16[1024,3584]{1,0:T(8,128)(2,1)} convert(f32[1024,3584]{1,0:T(8,128)} %reduce-scatter.6.cloned.1.call-done) | non-fusion elementwise | flops 3670016 | bytes 22020096 | tf_op jit(solution)/shard_map/convert_element_type | solution.py:93
  170.0 25.3 %reduce-scatter.4.cloned.1.call-done = f32[1024,3584]{1,0:T(8,128)} async-done(((f32[2048,3584]{1,0:T(8,128)}), f32[1024,3584]{1,0:T(8,128)}) %reduce-scatter.4.cloned.1.call-update) | async-done | bytes 14680080 | tf_op jit(solution)/shard_map/reduce_scatter | solution.py:86
  195.4 9.1 %convert_element_type.43 = bf16[1024,3584]{1,0:T(8,128)(2,1)} convert(f32[1024,3584]{1,0:T(8,128)} %reduce-scatter.4.cloned.1.call-done) | non-fusion elementwise | flops 3670016 | bytes 22020096 | tf_op jit(solution)/shard_map/convert_element_type | solution.py:92
  204.4 0.0 copy-done.1
  (7 shorter events, 0.1 us)
Async XLA Ops:
  7.2 2.7 %copy-start = (bf16[128,3584]{1,0:T(8,128)(2,1)S(1)}, bf16[128,3584]{1,0:T(8,128)(2,1)}, u32[]{:S(2)}) copy-start(bf16[128,3584]{1,0:T(8,128)(2,1)} %param.9) | copy-start | bytes 2752516
  10.9 20.3 %all-to-all-start.1 = ((bf16[8,8,3584]{2,1,0:T(8,128)(2,1)}), bf16[8,8,3584]{2,1,0:T(8,128)(2,1)S(1)}, u32[]{:S(2)}, u32[]{:S(2)}) async-start(bf16[8,8,3584]{2,1,0:T(8,128)(2,1)} %convolution_convert_fusion), calls=%async_computation.1 | async-start | bytes 917504 | tf_op jit(solution)/shard_map/all_to_all | solution.py:68
  31.2 23.0 %all-to-all-start = ((bf16[8,8,3584]{2,1,0:T(8,128)(2,1)}), bf16[8,8,3584]{2,1,0:T(8,128)(2,1)S(1)}, u32[]{:S(2)}, u32[]{:S(2)}) async-start(bf16[8,8,3584]{2,1,0:T(8,128)(2,1)} %fusion.1), calls=%async_computation | async-start | bytes 917504 | tf_op jit(solution)/shard_map/all_to_all | solution.py:69
  34.9 113.4 %reduce-scatter.8.cloned.1.call-start = ((), (), s32[]{:S(2)}) async-start(), calls=%async_computation.8 | async-start | bytes 44040192 | tf_op jit(solution)/shard_map/reduce_scatter | solution.py:88
  66.0 91.9 %reduce-scatter.6.cloned.1.call-start = ((), (), s32[]{:S(2)}) async-start(), calls=%async_computation.7 | async-start | bytes 44040192 | tf_op jit(solution)/shard_map/reduce_scatter | solution.py:87
  94.9 100.5 %reduce-scatter.4.cloned.1.call-start = ((), (), s32[]{:S(2)}) async-start(), calls=%async_computation.6 | async-start | bytes 44040192 | tf_op jit(solution)/shard_map/reduce_scatter | solution.py:86
  157.9 46.6 %copy-start.1 = (bf16[128,3584]{1,0:T(8,128)(2,1)S(1)}, bf16[128,3584]{1,0:T(8,128)(2,1)}, u32[]{:S(2)}) copy-start(bf16[128,3584]{1,0:T(8,128)(2,1)} %param.9) | copy-start | bytes 2752516
Sparse Core Ops, SparseCore 0:
  66.1 41.7 reduce-scatter.7
  110.1 41.4 reduce-scatter.5
  153.9 41.3 reduce-scatter.3
where the time goes:
time: 212 us; the launch traced here: 211 us
  matrix products  97.8 us (46%)
  waiting for transfers between devices  35.4 us (17%)
  other arithmetic  34.1 us (16%)
  blocking collectives  18.5 us (9%)
  between operations  13.8 us (7%)
  starting transfers between devices  11.2 us (5%)
    reduce_scatter x1, waiting for transfers between devices, per_device(): lax.psum_scatter(grad_terms[0], 'dp', scatter_dimension=0, tiled=True)  25.3 us
    dot_general x1, matrix products, expert_pass(): jnp.einsum('nh,nd->hd', grad_pre_up, in_tokens, preferred_element_type=jn...  19.1 us
    all_to_all x1, blocking collectives, per_device(): lax.all_to_all(partials.reshape(send_shape), 'expert', split_axis=0, conc...  18.5 us
    dot_general x1, matrix products, expert_pass(): jnp.einsum('nh,nd->hd', grad_pre_gate, in_tokens, preferred_element_type=...  15.1 us
    convert_element_type x1, other arithmetic, per_device(): summed[1].astype(jnp.bfloat16)  12.1 us
    dot_general x1, matrix products, expert_pass(): jnp.einsum('nh,nd->hd', activated, in_scaled, preferred_element_type=jnp....  11.7 us
    dot_general x1, matrix products, expert_pass(): jnp.dot(grad_pre_up, up_rows, preferred_element_type=jnp.float32)  10.4 us
    all_to_all x1, waiting for transfers between devices, per_device(): lax.all_to_all(replicate_rows(picked), 'expert', split_axis=0, concat_axi...  10 us
  transfers between devices with their start and end apart: 5, of which 2 were waited for; matrix products, arithmetic and copies ran while one was open for 51% of the time, Pallas kernels for 0%

commit v1 on v0

--- a/solution.py
+++ b/solution.py
@@ -5,6 +5,22 @@
 
 FLIGHT = 8
 HOTCAP = 8
+
+
+def pairwise_exchange(x, axis, split, join):
+    ways, here = (lax.axis_size(axis), lax.axis_index(axis))
+    width = x.shape[split] // ways
+    shape = list(x.shape)
+    shape[split] = width
+    height = shape[join]
+    shape[join] = height * ways
+    full = jnp.zeros(shape, x.dtype)
+    for mask in range(ways):
+        part = lax.dynamic_slice_in_dim(x, (here ^ mask) * width, width, axis=split)
+        if mask:
+            part = lax.ppermute(part, axis, [(d, d ^ mask) for d in range(ways)])
+        full = lax.dynamic_update_slice_in_dim(full, part, (here ^ mask) * height, axis=join)
+    return full
 
 
 def expert_pass(in_tokens, in_scaled, gate_rows, up_rows, down_rows):
@@ -65,7 +81,7 @@
         return widened.reshape(send_shape)
 
     got_tokens, got_scaled = (
-        lax.all_to_all(replicate_rows(picked), "expert", split_axis=0, concat_axis=0, tiled=True),
+        pairwise_exchange(replicate_rows(picked), "expert", 0, 0),
         lax.all_to_all(replicate_rows(scaled), "expert", split_axis=0, concat_axis=0, tiled=True),
     )
     partials, grad_terms = expert_pass(

time: 212 us -> 227 us (1.071)
  waiting for transfers between devices: 35.4 us -> 44 us
  starting transfers between devices: 11.2 us -> 19.4 us
    ppermute x0 -> x7, starting transfers between devices: none -> 14.2 us  [pairwise_exchange(): part = lax.ppermute(part, axis, [(d, d ^ mask) for d in range(ways)])]
    all_to_all x1 -> x0, waiting for transfers between devices: 10 us -> none  [per_device(): lax.all_to_all(replicate_rows(picked), 'expert', split_axis=0, concat_axi...]
    reduce_scatter x1, waiting for transfers between devices: 25.3 us -> 34.6 us  [per_device(): lax.psum_scatter(grad_terms[0], 'dp', scatter_dimension=0, tiled=True)]
    ppermute x0 -> x7, waiting for transfers between devices: none -> 8.07 us  [pairwise_exchange(): part = lax.ppermute(part, axis, [(d, d ^ mask) for d in range(ways)])]
    dot_general x1, matrix products: 19.1 us -> 11.8 us  [expert_pass(): jnp.einsum('nh,nd->hd', grad_pre_up, in_tokens, preferred_element_type=jn...]
    all_to_all x1 -> x0, starting transfers between devices: 7.25 us -> none  [per_device(): lax.all_to_all(replicate_rows(picked), 'expert', split_axis=0, concat_axi...]
    dot_general x1, matrix products: 11.7 us -> 15.6 us  [expert_pass(): jnp.einsum('nh,nd->hd', activated, in_scaled, preferred_element_type=jnp....]
    dot_general x1, matrix products: 15.1 us -> 18.9 us  [expert_pass(): jnp.einsum('nh,nd->hd', grad_pre_gate, in_tokens, preferred_element_type=...]
  transfers between devices with their start and end apart: 5 -> 11, of which waited for: 2 -> 4; matrix products, arithmetic and copies ran while one was open for 51% -> 43% of each run, Pallas kernels for 0% -> 0%
where the time goes in v1:
time: 227 us; the launch traced here: 226 us
  matrix products  96.7 us (43%)
  waiting for transfers between devices  44 us (19%)
  other arithmetic  34.1 us (15%)
  starting transfers between devices  19.4 us (9%)
  blocking collectives  17.9 us (8%)
  between operations  13.9 us (6%)
    reduce_scatter x1, waiting for transfers between devices, per_device(): lax.psum_scatter(grad_terms[0], 'dp', scatter_dimension=0, tiled=True)  34.6 us
    dot_general x1, matrix products, expert_pass(): jnp.einsum('nh,nd->hd', grad_pre_gate, in_tokens, preferred_element_type=...  18.9 us
    all_to_all x1, blocking collectives, per_device(): lax.all_to_all(partials.reshape(send_shape), 'expert', split_axis=0, conc...  17.9 us
    dot_general x1, matrix products, expert_pass(): jnp.einsum('nh,nd->hd', activated, in_scaled, preferred_element_type=jnp....  15.6 us
    ppermute x7, starting transfers between devices, pairwise_exchange(): part = lax.ppermute(part, axis, [(d, d ^ mask) for d in range(ways)])  14.2 us
    convert_element_type x1, other arithmetic, per_device(): summed[1].astype(jnp.bfloat16)  12.6 us
    dot_general x1, matrix products, expert_pass(): jnp.einsum('nh,nd->hd', grad_pre_up, in_tokens, preferred_element_type=jn...  11.8 us
    dot_general x1, matrix products, expert_pass(): jnp.einsum('nd,hd->nh', in_scaled, down_rows, preferred_element_type=jnp....  9.71 us
  transfers between devices with their start and end apart: 11, of which 4 were waited for; matrix products, arithmetic and copies ran while one was open for 43% of the time, Pallas kernels for 0%

profile of v1, /device:TPU:0, one launch (start us, length us, event | category | flops | bytes accessed | tf_op | source)
XLA Modules:
  0.0 226.4 jit_solution(6558546683668866942)
XLA Ops:
  7.2 0.0 copy-start
  7.2 0.7 broadcast_compare_fusion.1
  8.0 0.7 select_reduce_fusion.2
  8.7 0.8 and_select_fusion
  9.5 0.1 copy.28
  9.6 0.2 reduce_window_sum.11
  9.9 0.3 convolution_convert_fusion
  10.2 0.1 constant_dynamic-slice_fusion.6
  10.2 3.0 %collective-permute-start = (bf16[1,8,3584]{2,1,0:T(8,128)(2,1)S(1)}, bf16[1,8,3584]{2,1,0:T(8,128)(2,1)S(1)}, u32[]{:S(2)}, u32[]{:S(2)}) collective-permute-start(bf16[1,8,3584]{2,1,0:T(8,128)(2,1)S(1)} %get-tuple-element.12), channel_id=1, source_target_pairs={{0,2},{2,0},{4,6},{6,4},{8,10},{10,8},{12,14},{14,12},{1,3},{3,1},... | collective-permute-start | bytes 172040 | tf_op jit(solution)/shard_map/ppermute | solution.py:21
  13.2 1.6 collective-permute-start.1
  14.8 0.0 collective-permute-start.2
  14.8 3.0 %collective-permute-start.3 = (bf16[1,8,3584]{2,1,0:T(8,128)(2,1)S(1)}, bf16[1,8,3584]{2,1,0:T(8,128)(2,1)S(1)}, u32[]{:S(2)}, u32[]{:S(2)}) collective-permute-start(bf16[1,8,3584]{2,1,0:T(8,128)(2,1)S(1)} %get-tuple-element.9), channel_id=1, source_target_pairs={{0,8},{2,10},{4,12},{6,14},{8,0},{10,2},{12,4},{14,6},{1,9},{3,11}... | collective-permute-start | bytes 172040 | tf_op jit(solution)/shard_map/ppermute | solution.py:21
  17.8 1.3 collective-permute-start.4
  19.1 0.7 select_reduce_fusion.1
  19.8 0.1 select_reduce_fusion
  19.9 0.1 copy.31
  20.0 2.2 fusion.1
  22.2 4.9 %all-to-all-start = ((bf16[8,8,3584]{2,1,0:T(8,128)(2,1)}), bf16[8,8,3584]{2,1,0:T(8,128)(2,1)S(1)}, u32[]{:S(2)}, u32[]{:S(2)}) async-start(bf16[8,8,3584]{2,1,0:T(8,128)(2,1)} %fusion.1), calls=%async_computation | async-start | bytes 917504 | tf_op jit(solution)/shard_map/all_to_all | solution.py:85
  27.1 0.0 reduce-scatter.6.cloned.1.call-start
  27.1 0.0 collective-permute-done
  27.1 3.8 %collective-permute-start.5 = (bf16[1,8,3584]{2,1,0:T(8,128)(2,1)S(1)}, bf16[1,8,3584]{2,1,0:T(8,128)(2,1)S(1)}, u32[]{:S(2)}, u32[]{:S(2)}) collective-permute-start(bf16[1,8,3584]{2,1,0:T(8,128)(2,1)S(1)} %get-tuple-element.7), channel_id=1, source_target_pairs={{0,12},{2,14},{4,8},{6,10},{8,4},{10,6},{12,0},{14,2},{1,13},{3,15... | collective-permute-start | bytes 172040 | tf_op jit(solution)/shard_map/ppermute | solution.py:21
  31.0 0.0 collective-permute-done.1
  31.0 1.5 collective-permute-start.6
  32.5 0.0 collective-permute-done.2
  32.5 0.0 collective-permute-done.3
  32.6 6.5 %collective-permute-done.5 = bf16[1,8,3584]{2,1,0:T(8,128)(2,1)S(1)} collective-permute-done((bf16[1,8,3584]{2,1,0:T(8,128)(2,1)S(1)}, bf16[1,8,3584]{2,1,0:T(8,128)(2,1)S(1)}, u32[]{:S(2)}, u32[]{:S(2)}) %collective-permute-start.5) | collective-permute-done | bytes 57376 | tf_op jit(solution)/shard_map/ppermute | solution.py:21
  39.1 1.6 collective-permute-done.6
  40.6 9.7 %fusion.11 = f32[64,2048]{1,0:T(8,128)S(1)} fusion(bf16[2048,3584]{1,0:T(8,128)(2,1)} %param.15, bf16[8,8,3584]{2,1,0:T(8,128)(2,1)S(1)} %constant_dynamic-update-slice_fusion.6), kind=kOutput, calls=%fused_computation.19 | convolution fusion | flops 939524096 | bytes 15663104 | tf_op jit(solution)/shard_map/nd,hd->nh/dot_general | solution.py:27
  50.3 9.7 %fusion.13 = f32[64,2048]{1,0:T(8,128)S(1)} fusion(bf16[2048,3584]{1,0:T(8,128)(2,1)} %param.16, bf16[8,8,3584]{2,1,0:T(8,128)(2,1)S(1)} %constant_dynamic-update-slice_fusion.6), kind=kOutput, calls=%fused_computation.21 | convolution fusion | flops 939524096 | bytes 15663104 | tf_op jit(solution)/shard_map/nd,hd->nh/dot_general | solution.py:28
  60.0 0.0 all-to-all-done
  60.0 9.7 %multiply_convert_fusion.1 = (bf16[64,2048]{1,0:T(8,128)(2,1)S(1)}, bf16[64,2048]{1,0:T(8,128)(2,1)S(1)}) fusion(f32[64,2048]{1,0:T(8,128)S(1)} %fusion.11, f32[64,2048]{1,0:T(8,128)S(1)} %fusion.13, bf16[2048,3584]{1,0:T(8,128)(2,1)} %param.17, bf16[8,8,3584]{2,1,0:T(8,128)(2,1)S(1)} %all-to-all-done), kind=kOutput, calls=%fused_computation.11 | convolution fusion | flops 941228032 | bytes 16711680 | tf_op jit(solution)/shard_map/nd,hd->nh/dot_general | solution.py:32
  69.7 11.8 %fusion.7 = f32[2048,3584]{1,0:T(8,128)} fusion(bf16[64,2048]{1,0:T(8,128)(2,1)S(1)} %get-tuple-element.4, bf16[8,8,3584]{2,1,0:T(8,128)(2,1)S(1)} %constant_dynamic-update-slice_fusion.6), kind=kOutput, calls=%fused_computation.15 | convolution fusion | flops 939524096 | bytes 30081024 | tf_op jit(solution)/shard_map/nh,nd->hd/dot_general | solution.py:40
  81.5 0.0 reduce-scatter.6.cloned.1.call-update
  81.5 0.2 reduce-scatter.8.cloned.1.call-start
  81.7 15.6 %fusion.15 = f32[2048,3584]{1,0:T(8,128)} fusion(bf16[8,8,3584]{2,1,0:T(8,128)(2,1)S(1)} %all-to-all-done, f32[64,2048]{1,0:T(8,128)S(1)} %fusion.13, f32[64,2048]{1,0:T(8,128)S(1)} %fusion.11), kind=kOutput, calls=%fused_computation.23 | convolution fusion | flops 940310528 | bytes 30867456 | tf_op jit(solution)/shard_map/nh,nd->hd/dot_general | solution.py:41
  97.4 0.0 reduce-scatter.8.cloned.1.call-update
  97.4 0.0 reduce-scatter.4.cloned.1.call-start
  97.4 18.9 %fusion.9 = f32[2048,3584]{1,0:T(8,128)} fusion(bf16[64,2048]{1,0:T(8,128)(2,1)S(1)} %get-tuple-element.5, bf16[8,8,3584]{2,1,0:T(8,128)(2,1)S(1)} %constant_dynamic-update-slice_fusion.6), kind=kOutput, calls=%fused_computation.17 | convolution fusion | flops 939524096 | bytes 30081024 | tf_op jit(solution)/shard_map/nh,nd->hd/dot_general | solution.py:37
  116.4 0.0 reduce-scatter.4.cloned.1.call-update
  116.4 9.6 %fusion.27 = f32[64,3584]{1,0:T(8,128)S(1)} fusion(bf16[64,2048]{1,0:T(8,128)(2,1)S(1)} %get-tuple-element.5, bf16[2048,3584]{1,0:T(8,128)(2,1)} %param.15), kind=kOutput, calls=%fused_computation.59 | convolution fusion | flops 939524096 | bytes 15859712 | tf_op jit(solution)/shard_map/dot_general | solution.py:42
  126.0 7.8 %fusion.3 = bf16[8,8,3584]{2,1,0:T(8,128)(2,1)S(1)} fusion(f32[64,3584]{1,0:T(8,128)S(1)} %fusion.27, bf16[64,2048]{1,0:T(8,128)(2,1)S(1)} %get-tuple-element.4, bf16[2048,3584]{1,0:T(8,128)(2,1)} %param.16), kind=kOutput, calls=%fused_computation.7 | convolution fusion | flops 939982848 | bytes 16318464 | tf_op jit(solution)/shard_map/dot_general | solution.py:44
  133.8 17.9 %all_to_all.10 = bf16[8,8,3584]{2,1,0:T(8,128)(2,1)S(1)} all-to-all(bf16[8,8,3584]{2,1,0:T(8,128)(2,1)S(1)} %fusion.3), channel_id=1, replica_groups=mesh['groups'=2,'expert'=8,'dp'=2] {'expert'}, dimensions={0} | all-to-all | bytes 917504 | tf_op jit(solution)/shard_map/all_to_all | solution.py:94
  151.8 1.4 fusion
  153.1 12.6 %convert_element_type.44 = bf16[1024,3584]{1,0:T(8,128)(2,1)} convert(f32[1024,3584]{1,0:T(8,128)} %reduce-scatter.6.cloned.1.call-done) | non-fusion elementwise | flops 3670016 | bytes 22020096 | tf_op jit(solution)/shard_map/convert_element_type | solution.py:109
  165.7 1.3 reduce-scatter.8.cloned.1.call-done
  167.0 9.2 %convert_element_type.46 = bf16[1024,3584]{1,0:T(8,128)(2,1)} convert(f32[1024,3584]{1,0:T(8,128)} %reduce-scatter.8.cloned.1.call-done) | non-fusion elementwise | flops 3670016 | bytes 22020096 | tf_op jit(solution)/shard_map/convert_element_type | solution.py:110
  176.2 34.6 %reduce-scatter.4.cloned.1.call-done = f32[1024,3584]{1,0:T(8,128)} async-done(((f32[2048,3584]{1,0:T(8,128)}), f32[1024,3584]{1,0:T(8,128)}) %reduce-scatter.4.cloned.1.call-update) | async-done | bytes 14680080 | tf_op jit(solution)/shard_map/reduce_scatter | solution.py:102
  210.8 9.1 %convert_element_type.43 = bf16[1024,3584]{1,0:T(8,128)(2,1)} convert(f32[1024,3584]{1,0:T(8,128)} %reduce-scatter.4.cloned.1.call-done) | non-fusion elementwise | flops 3670016 | bytes 22020096 | tf_op jit(solution)/shard_map/convert_element_type | solution.py:108
  (20 shorter events, 0.2 us)
Async XLA Ops:
  7.2 2.7 %copy-start = (bf16[128,3584]{1,0:T(8,128)(2,1)S(1)}, bf16[128,3584]{1,0:T(8,128)(2,1)}, u32[]{:S(2)}) copy-start(bf16[128,3584]{1,0:T(8,128)(2,1)} %param.9) | copy-start | bytes 2752516
  10.2 16.9 %collective-permute-start = (bf16[1,8,3584]{2,1,0:T(8,128)(2,1)S(1)}, bf16[1,8,3584]{2,1,0:T(8,128)(2,1)S(1)}, u32[]{:S(2)}, u32[]{:S(2)}) collective-permute-start(bf16[1,8,3584]{2,1,0:T(8,128)(2,1)S(1)} %get-tuple-element.12), channel_id=1, source_target_pairs={{0,2},{2,0},{4,6},{6,4},{8,10},{10,8},{12,14},{14,12},{1,3},{3,1},... | collective-permute-start | bytes 172040 | tf_op jit(solution)/shard_map/ppermute | solution.py:21
  13.2 17.7 %collective-permute-start.1 = (bf16[1,8,3584]{2,1,0:T(8,128)(2,1)S(1)}, bf16[1,8,3584]{2,1,0:T(8,128)(2,1)S(1)}, u32[]{:S(2)}, u32[]{:S(2)}) collective-permute-start(bf16[1,8,3584]{2,1,0:T(8,128)(2,1)S(1)} %get-tuple-element.11), channel_id=1, source_target_pairs={{0,4},{2,6},{4,0},{6,2},{8,12},{10,14},{12,8},{14,10},{1,5},{3,7},... | collective-permute-start | bytes 172040 | tf_op jit(solution)/shard_map/ppermute | solution.py:21
  14.8 17.7 %collective-permute-start.2 = (bf16[1,8,3584]{2,1,0:T(8,128)(2,1)S(1)}, bf16[1,8,3584]{2,1,0:T(8,128)(2,1)S(1)}, u32[]{:S(2)}, u32[]{:S(2)}) collective-permute-start(bf16[1,8,3584]{2,1,0:T(8,128)(2,1)S(1)} %get-tuple-element.10), channel_id=1, source_target_pairs={{0,6},{2,4},{4,2},{6,0},{8,14},{10,12},{12,10},{14,8},{1,7},{3,5},... | collective-permute-start | bytes 172040 | tf_op jit(solution)/shard_map/ppermute | solution.py:21
  14.8 17.7 %collective-permute-start.3 = (bf16[1,8,3584]{2,1,0:T(8,128)(2,1)S(1)}, bf16[1,8,3584]{2,1,0:T(8,128)(2,1)S(1)}, u32[]{:S(2)}, u32[]{:S(2)}) collective-permute-start(bf16[1,8,3584]{2,1,0:T(8,128)(2,1)S(1)} %get-tuple-element.9), channel_id=1, source_target_pairs={{0,8},{2,10},{4,12},{6,14},{8,0},{10,2},{12,4},{14,6},{1,9},{3,11}... | collective-permute-start | bytes 172040 | tf_op jit(solution)/shard_map/ppermute | solution.py:21
  17.8 14.7 %collective-permute-start.4 = (bf16[1,8,3584]{2,1,0:T(8,128)(2,1)S(1)}, bf16[1,8,3584]{2,1,0:T(8,128)(2,1)S(1)}, u32[]{:S(2)}, u32[]{:S(2)}) collective-permute-start(bf16[1,8,3584]{2,1,0:T(8,128)(2,1)S(1)} %get-tuple-element.8), channel_id=1, source_target_pairs={{0,10},{2,8},{4,14},{6,12},{8,2},{10,0},{12,6},{14,4},{1,11},{3,9}... | collective-permute-start | bytes 172040 | tf_op jit(solution)/shard_map/ppermute | solution.py:21
  22.2 37.8 %all-to-all-start = ((bf16[8,8,3584]{2,1,0:T(8,128)(2,1)}), bf16[8,8,3584]{2,1,0:T(8,128)(2,1)S(1)}, u32[]{:S(2)}, u32[]{:S(2)}) async-start(bf16[8,8,3584]{2,1,0:T(8,128)(2,1)} %fusion.1), calls=%async_computation | async-start | bytes 917504 | tf_op jit(solution)/shard_map/all_to_all | solution.py:85
  27.1 126.1 %reduce-scatter.6.cloned.1.call-start = ((), (), s32[]{:S(2)}) async-start(), calls=%async_computation.6 | async-start | bytes 44040192 | tf_op jit(solution)/shard_map/reduce_scatter | solution.py:103
  27.1 12.0 %collective-permute-start.5 = (bf16[1,8,3584]{2,1,0:T(8,128)(2,1)S(1)}, bf16[1,8,3584]{2,1,0:T(8,128)(2,1)S(1)}, u32[]{:S(2)}, u32[]{:S(2)}) collective-permute-start(bf16[1,8,3584]{2,1,0:T(8,128)(2,1)S(1)} %get-tuple-element.7), channel_id=1, source_target_pairs={{0,12},{2,14},{4,8},{6,10},{8,4},{10,6},{12,0},{14,2},{1,13},{3,15... | collective-permute-start | bytes 172040 | tf_op jit(solution)/shard_map/ppermute | solution.py:21
  31.0 9.7 %collective-permute-start.6 = (bf16[1,8,3584]{2,1,0:T(8,128)(2,1)S(1)}, bf16[1,8,3584]{2,1,0:T(8,128)(2,1)S(1)}, u32[]{:S(2)}, u32[]{:S(2)}) collective-permute-start(bf16[1,8,3584]{2,1,0:T(8,128)(2,1)S(1)} %get-tuple-element.6), channel_id=1, source_target_pairs={{0,14},{2,12},{4,10},{6,8},{8,6},{10,4},{12,2},{14,0},{1,15},{3,13... | collective-permute-start | bytes 172040 | tf_op jit(solution)/shard_map/ppermute | solution.py:21
  81.5 85.5 %reduce-scatter.8.cloned.1.call-start = ((), (), s32[]{:S(2)}) async-start(), calls=%async_computation.7 | async-start | bytes 44040192 | tf_op jit(solution)/shard_map/reduce_scatter | solution.py:104
  97.4 113.4 %reduce-scatter.4.cloned.1.call-start = ((), (), s32[]{:S(2)}) async-start(), calls=%async_computation.5 | async-start | bytes 44040192 | tf_op jit(solution)/shard_map/reduce_scatter | solution.py:102
  167.0 52.8 %copy-start.1 = (bf16[128,3584]{1,0:T(8,128)(2,1)S(1)}, bf16[128,3584]{1,0:T(8,128)(2,1)}, u32[]{:S(2)}) copy-start(bf16[128,3584]{1,0:T(8,128)(2,1)} %param.9) | copy-start | bytes 2752516
Sparse Core Ops, SparseCore 0:
  81.6 41.4 reduce-scatter.5
  125.4 41.5 reduce-scatter.7
  169.3 41.3 reduce-scatter.3
